TPU v7x, 256 devices: a whole 4x4x8 slice. The times are simulated.
256 devices in a mesh: env: 4 (over x_lo, core), tm: 64 (over x_hi, z, y).
Axes of the slice: x: 4 (x_hi: 2, x_lo: 2; x = x_hi * 2 + x_lo), y: 4, z: 8, core: 2. Of those that a mesh axis runs over, the one named last changes fastest.
Arguments:
- hidden: bfloat16 [4, 64, 256, 1024], P('env', 'tm'), may hold values from -6 to 6
- done_step: int32 [4, 64], P('env', 'tm'), may hold values from 0 to 255
- alive: int32 [4, 64, 256], P('env', None, 'tm'), may hold values 0 or 1
- targets: float32 [4, 64, 256], P('env', None, 'tm'), may hold values from -6 to 6
- gain_t: float32 [1024], replicated, may hold values from 0.25 to 1.75
- w_qkv_t: bfloat16 [1024, 3072], replicated, may hold values from -5 to 5
- w_out_t: bfloat16 [1024, 1024], replicated, may hold values from -0.1875 to 0.1875
- gain_a: float32 [1024], replicated, may hold values from 0.25 to 1.75
- w_qkv_a: bfloat16 [1024, 3072], P('tm'), may hold values from -5 to 5
- w_out_a: bfloat16 [1024, 1024], P('tm'), may hold values from -0.1875 to 0.1875
- w_value: float32 [1024], replicated, may hold values from -0.1875 to 0.1875
Outputs:
- values: float32 [4, 64, 256], P('env', None, 'tm')
- input_grad: bfloat16 [4, 64, 256, 1024], P('env', 'tm')
- qkv_grad: float32 [1024, 3072], P('tm')
- out_grad: float32 [1024, 1024], P('tm')
Inputs may be any that keep to these rules, and one draw needn't show every extreme that they name: `done_step`: the last step of an agent's first episode in the window; later steps form a new episode.
All inputs are finite; a program needn't handle non-finite values. No bound on the sum of `alive` on one device may be relied on, other than what follows from the above.
Results may differ from a plain program's by a relative error of at most 0.02.
Values may be sent and summed in bfloat16 or wider, within the bound.
A program may use at most 128 MiB of HBM per device.

v0:
```python
import math
import jax
import jax.numpy as jnp
from jax import lax
from jax.sharding import PartitionSpec as P

HEADS = 8
HI = lax.Precision.HIGHEST


def norm_scale(rows, gain):
    return rows * lax.rsqrt(jnp.mean(rows * rows, axis=-1, keepdims=True) + 1e-06) * gain


def attend(qkv, allowed, head_count):
    width = qkv.shape[-1] // 3
    size = width // head_count
    shape = qkv.shape[:-1] + (head_count, size)
    queries = qkv[..., :width].reshape(shape)
    key_rows = qkv[..., width : 2 * width].reshape(shape)
    value_rows = qkv[..., 2 * width :].reshape(shape)
    scores = jnp.einsum("qhe,khe->hqk", queries, key_rows, preferred_element_type=jnp.float32)
    scores = jnp.where(allowed[None], scores / math.sqrt(size), -1e30)
    row_max = jnp.max(scores, axis=-1, keepdims=True)
    weights = jnp.exp(scores - row_max)
    probs = (weights / jnp.sum(weights, axis=-1, keepdims=True)).astype(jnp.bfloat16)
    mixed = jnp.einsum("hqk,khe->qhe", probs, value_rows, preferred_element_type=jnp.float32)
    return mixed.reshape(qkv.shape[:-1] + (width,))


def temporal_block(rows, done, gain, w_qkv, w_out, head_count):
    length, width = rows.shape
    rows_f = rows.astype(jnp.float32)
    normed = norm_scale(rows_f, gain).astype(jnp.bfloat16)
    qkv = jnp.dot(normed, w_qkv, preferred_element_type=jnp.float32).astype(jnp.bfloat16)
    positions = jnp.arange(length, dtype=jnp.int32)
    later = positions > done
    allowed = (positions[:, None] >= positions[None, :]) & (later[:, None] == later[None, :])
    mixed = attend(qkv, allowed, head_count).astype(jnp.bfloat16)
    added = jnp.dot(mixed, w_out, preferred_element_type=jnp.float32)
    return (rows_f + added).astype(jnp.bfloat16)


def left_product(left, right):
    return lax.dot_general(
        left, right, (((0,), (0,)), ((), ())), preferred_element_type=jnp.float32
    )


def agent_step(lifted, alive_rows, target_rows, gain, w_qk, z, w_value, head_count):
    agent_count, step_count, width = lifted.shape
    size = width // head_count
    lifted_f = lifted.astype(jnp.float32)
    normed_f, norm_pull = jax.vjp(lambda rows: norm_scale(rows, gain), lifted_f)
    normed = normed_f.astype(jnp.bfloat16).reshape(-1, width)
    qk = jnp.dot(normed, w_qk, preferred_element_type=jnp.float32).astype(jnp.bfloat16)
    qk = qk.reshape(agent_count, step_count, 2, head_count, size)
    q, k = (qk[:, :, 0], qk[:, :, 1])
    s = jnp.dot(normed.astype(jnp.float32), z, precision=HI)
    s = s.reshape(agent_count, step_count, head_count).transpose(1, 2, 0)
    living = alive_rows.T == 1
    allowed = living[:, None, :] | jnp.eye(agent_count, dtype=bool)[None]
    scores = jnp.einsum("qbhe,kbhe->bhqk", q, k, preferred_element_type=jnp.float32)
    scores = jnp.where(allowed[:, None], scores / math.sqrt(size), -1e30)
    weights = jnp.exp(scores - jnp.max(scores, axis=-1, keepdims=True))
    probs = weights / jnp.sum(weights, axis=-1, keepdims=True)
    pv = jnp.sum(probs * s[:, :, None, :], axis=-1)
    predicted = jnp.sum(lifted_f * w_value, axis=-1) + jnp.sum(pv, axis=1).T
    err = 32.0 * alive_rows.astype(jnp.float32) * (predicted - target_rows)
    weighted = probs * err.T[:, None, :, None]
    t = jnp.sum(weighted, axis=2)
    ds = weighted * (s[:, :, None, :] - pv[..., None]) * (1.0 / math.sqrt(size))
    ds = ds.astype(jnp.bfloat16)
    dq = jnp.einsum("bhqk,kbhe->qbhe", ds, k, preferred_element_type=jnp.float32)
    dk = jnp.einsum("bhqk,qbhe->kbhe", ds, q, preferred_element_type=jnp.float32)
    dqk = jnp.stack([dq, dk], axis=2).astype(jnp.bfloat16).reshape(-1, 2 * width)
    t = t.transpose(2, 0, 1).reshape(-1, head_count)
    grad_normed = jnp.dot(dqk, w_qk.T, preferred_element_type=jnp.float32)
    grad_normed = grad_normed + jnp.dot(t, z.T, precision=HI)
    grad_top = err[..., None] * w_value
    grad_lifted = grad_top + norm_pull(grad_normed.reshape(agent_count, step_count, width))[0]
    return (predicted, grad_lifted.astype(jnp.bfloat16), normed, dqk, t)


def per_device(
    hidden, done_step, alive, targets, gain_t, w_qkv_t, w_out_t, gain_a, w_qkv_a, w_out_a, w_value
):
    width = hidden.shape[-1]
    size = width // HEADS
    local_rows = hidden[0, 0]
    done = done_step[0, 0]
    v = lax.all_gather(
        jnp.sum(w_out_a.astype(jnp.float32) * w_value, axis=1), "tm", axis=0, tiled=True
    )
    w_v = w_qkv_a[:, 2 * width :].astype(jnp.float32)
    z = jnp.sum((w_v * v).reshape(-1, HEADS, size), axis=-1)
    z = lax.all_gather(z, "tm", axis=0, tiled=True)
    w_qk = lax.all_gather(w_qkv_a[:, : 2 * width], "tm", axis=0, tiled=True)
    first, pull = jax.vjp(
        lambda rows: temporal_block(rows, done, gain_t, w_qkv_t, w_out_t, HEADS), local_rows
    )
    lifted = lax.all_to_all(first[None], "tm", split_axis=1, concat_axis=0, tiled=True)
    predicted, grad_lifted, normed, dqk, t = agent_step(
        lifted, alive[0], targets[0], gain_a, w_qk, z, w_value, HEADS
    )
    returned = lax.all_to_all(grad_lifted, "tm", split_axis=0, concat_axis=1, tiled=True)
    terms = left_product(normed, dqk).astype(jnp.bfloat16)
    u_terms = lax.dot_general(normed.astype(jnp.float32), t, (((0,), (0,)), ((), ())), precision=HI)
    summed = lax.psum_scatter(terms, "tm", scatter_dimension=0, tiled=True)
    qk_grad = lax.psum(summed, "env").astype(jnp.float32)
    u_mine = lax.psum(u_terms, ("env", "tm"))
    u_mine = lax.dynamic_slice_in_dim(u_mine, lax.axis_index("tm") * w_v.shape[0], w_v.shape[0], 0)
    u_wide = jnp.repeat(u_mine, size, axis=1)
    v_grad = u_wide * v
    mixed_err = lax.psum(jnp.sum(u_wide * w_v, axis=0), "tm")
    mixed_err = lax.dynamic_slice_in_dim(
        mixed_err, lax.axis_index("tm") * w_out_a.shape[0], w_out_a.shape[0], 0
    )
    out_grad = mixed_err[:, None] * w_value
    qkv_grad = jnp.concatenate([qk_grad, v_grad], axis=1)
    input_grad = pull(returned[0])[0]
    return (predicted[None], input_grad[None, None], qkv_grad, out_grad)


def solution(mesh):
    in_specs = (
        P("env", "tm", None, None),
        P("env", "tm"),
        P("env", None, "tm"),
        P("env", None, "tm"),
        P(),
        P(),
        P(),
        P(),
        P("tm", None),
        P("tm", None),
        P(),
    )
    out_specs = (P("env", None, "tm"), P("env", "tm", None, None), P("tm", None), P("tm", None))
    return jax.shard_map(
        per_device, mesh=mesh, in_specs=in_specs, out_specs=out_specs, check_vma=False
    )
```

profile of v0, /device:TPU:1, one launch (start us, length us, event | category | flops | bytes accessed | tf_op | source)
XLA Modules:
  0.0 856.8 jit_solution(7488116643575696525)
XLA Ops:
  7.2 1.6 slice.24
  9.5 1.2 fusion.49
  10.7 0.5 copy-done.25
  11.3 4.9 convolution_convert_fusion
  16.1 1.1 slice_bitcast_fusion
  17.2 1.4 copy.98
  18.7 2.2 copy.97
  21.0 1.6 fusion.114
  23.3 0.7 copy-done.1
  24.0 1.0 copy-done.3
  25.4 0.7 fusion.37
  26.1 0.8 copy.135
  27.0 0.5 broadcast.202
  27.5 4.5 reduce.4
  32.0 2.2 reshape.279
  34.2 15.1 %all-to-all-start = ((bf16[64,2,2048]{2,1,0:T(2,128)(2,1)}), bf16[64,2,2048]{2,1,0:T(2,128)(2,1)S(1)}, u32[]{:S(2)}, u32[]{:S(2)}) async-start(bf16[64,2,2048]{2,1,0:T(2,128)(2,1)} %reshape.279), calls=%async_computation | async-start | bytes 1048576 | tf_op jit(solution)/shard_map/all_to_all | solution.py:102
  49.4 0.6 dynamic-slice
  51.0 156.9 %all-reduce.3 = f32[1024]{0:T(1024)S(1)} all-reduce(f32[1024]{0:T(1024)S(1)} %dynamic-update-slice), channel_id=1, replica_groups=mesh['env'=4,'tm'=64] {'tm'}, use_global_device_ids=true, to_apply=%add.3 | all-reduce | flops 1024 | bytes 8192
  207.9 0.8 fusion.93
  208.9 148.0 %all-gather = f32[64,16,8]{1,2,0:T(8,128)S(1)} all-gather(f32[1,16,8]{1,2,0:T(8,128)S(1)} %bitcast.169), channel_id=1, replica_groups=mesh['env'=4,'tm'=64] {'tm'}, dimensions={0}, use_global_device_ids=true | all-gather | bytes 33280 | tf_op jit(solution)/shard_map/all_gather | solution.py:97
  357.2 0.7 broadcast_or_fusion
  357.9 1.8 reshape.280
  359.7 1.6 fusion.39
  361.5 0.7 copy.75
  362.2 1.3 reshape.268
  363.5 1.5 multiply_convert_fusion
  365.0 0.8 copy-done.6
  365.8 1.3 convolution_bitcast_fusion.3
  367.1 3.5 fusion.16
  370.9 1.0 fusion.113
  371.9 3.5 multiply_reduce_fusion.2
  375.4 1.3 fusion.95
  376.7 3.3 convolution_bitcast_fusion
  380.0 3.4 convolution_bitcast_fusion.1
  383.5 1.3 maximum_convert_fusion
  384.8 1.7 copy.78
  386.4 2.3 convert_element_type.173
  388.7 4.6 convolution_convert_fusion.1
  393.5 0.5 copy-done.22
  394.1 1.6 multiply_reduce_fusion
  395.8 3.8 fusion.115
  399.6 2.1 fusion.40
  401.8 2.6 reshape.260
  404.4 2.8 fusion.47
  407.2 4.9 all-to-all-start.1
  412.1 1.5 convolution_bitcast_fusion.2
  413.6 132.2 %psum.22 = f32[1024,8]{0,1:T(8,128)S(1)} all-reduce(f32[1024,8]{0,1:T(8,128)S(1)} %convolution_bitcast_fusion.2), channel_id=1, replica_groups=mesh['env'=4,'tm'=64] {'env','tm'}, use_global_device_ids=true, to_apply=%region_19.20 | all-reduce | flops 8192 | bytes 65536 | tf_op jit(solution)/shard_map/psum | solution.py:111
  546.0 0.8 fusion.94
  546.8 156.0 %psum.23 = f32[1024]{0:T(1024)S(1)} all-reduce(f32[1024]{0:T(1024)S(1)} %get-tuple-element.19), channel_id=1, replica_groups=mesh['env'=4,'tm'=64] {'tm'}, use_global_device_ids=true, to_apply=%region_21.22 | all-reduce | flops 1024 | bytes 8192 | tf_op jit(solution)/shard_map/psum | solution.py:115
  702.9 0.7 broadcast_multiply_fusion
  703.6 0.9 squeeze.21
  704.6 2.6 convolution_convert_fusion.5
  707.2 1.2 copy.94
  708.5 2.3 fusion.6
  710.9 1.0 convert_reduce_fusion
  712.6 1.2 fusion.25
  713.8 1.2 fusion.24
  715.2 0.7 slice-done.1
  716.0 2.9 fusion.52
  718.9 45.1 %reduce-scatter.2.cloned.1.call-done = bf16[16,2048]{1,0:T(8,128)(2,1)} async-done(((bf16[1024,2048]{1,0:T(8,128)(2,1)}), bf16[16,2048]{1,0:T(8,128)(2,1)}) %reduce-scatter.2.cloned.1.call-update) | async-done | bytes 65552 | tf_op jit(solution)/shard_map/reduce_scatter | solution.py:109
  764.1 2.3 fusion.67
  766.4 82.4 %all-reduce.6.cloned.1.call-done = bf16[16,2048]{1,0:T(8,128)(2,1)} async-done(((bf16[16,2048]{1,0:T(8,128)(2,1)}), bf16[16,2048]{1,0:T(8,128)(2,1)}) %all-reduce.6.cloned.1.call-update) | async-done | bytes 65552 | tf_op jit(solution)/shard_map/psum | solution.py:110
  848.8 0.8 convert_element_type.192
  849.6 0.7 pad_maximum_fusion
  (107 shorter events, 4.4 us)
Async XLA Ops:
  7.2 18.2 %copy-start = (bf16[1024,1024]{1,0:T(8,128)(2,1)S(1)}, bf16[1024,1024]{1,0:T(8,128)(2,1)}, u32[]{:S(2)}) copy-start(bf16[1024,1024]{1,0:T(8,128)(2,1)} %param.17) | copy-start | bytes 6291460
  7.2 359.9 %all-gather.3.cloned.1.call-start = ((), (), s32[]{:S(2)}) async-start(), calls=%async_computation.3 | async-start | bytes 4259840 | tf_op jit(solution)/shard_map/all_gather | solution.py:98
  10.7 0.5 copy-start.25
  11.3 4.9 copy-start.28
  17.2 6.8 copy-start.9
  18.7 3.9 copy-start.11
  22.6 1.4 copy-start.1
  22.9 2.4 copy-start.16
  22.9 2.4 copy-start.7
  24.0 1.0 copy-start.3
  26.9 22.4 %copy-start.31 = (u32[256]{0:T(256)S(1)}, u32[256]{0:T(256)}, u32[]{:S(2)}) copy-start(u32[256]{0:T(256)} %constant.61) | copy-start | bytes 3076
  26.9 23.7 %copy-start.18 = (f32[1024]{0:T(1024)S(1)}, f32[1024]{0:T(1024)}, u32[]{:S(2)}) copy-start(f32[1024]{0:T(1024)} %param.21) | copy-start | bytes 12292
  27.0 23.7 %copy-start.21 = (bf16[16,1024]{1,0:T(8,128)(2,1)S(1)}, bf16[16,1024]{1,0:T(8,128)(2,1)}, u32[]{:S(2)}) copy-start(bf16[16,1024]{1,0:T(8,128)(2,1)} %param.20) | copy-start | bytes 98308
  32.0 325.1 %copy-start.27 = (s32[1,64,4]{1,2,0:T(4,128)S(1)}, s32[1,64,4]{1,2,0:T(4,128)}, u32[]{:S(2)}) copy-start(s32[1,64,4]{1,2,0:T(4,128)} %param.13) | copy-start | bytes 3076
  34.2 323.7 %all-to-all-start = ((bf16[64,2,2048]{2,1,0:T(2,128)(2,1)}), bf16[64,2,2048]{2,1,0:T(2,128)(2,1)S(1)}, u32[]{:S(2)}, u32[]{:S(2)}) async-start(bf16[64,2,2048]{2,1,0:T(2,128)(2,1)} %reshape.279), calls=%async_computation | async-start | bytes 1048576 | tf_op jit(solution)/shard_map/all_to_all | solution.py:102
  49.3 714.7 %reduce-scatter.2.cloned.1.call-start = ((), (), s32[]{:S(2)}) async-start(), calls=%async_computation.4 | async-start | bytes 4259840 | tf_op jit(solution)/shard_map/reduce_scatter | solution.py:109
  207.9 149.2 %copy-start.19 = (f32[1024]{0:T(1024)}, f32[1024]{0:T(1024)S(1)}, u32[]{:S(2)}) copy-start(f32[1024]{0:T(1024)S(1)} %all-reduce.3) | copy-start | bytes 12292
  357.9 5.6 copy-start.15
  361.3 9.4 %copy-start.23 = (f32[256]{0:T(256)}, f32[256]{0:T(256)S(1)}, u32[]{:S(2)}) copy-start(f32[256]{0:T(256)S(1)} %get-tuple-element.24) | copy-start | bytes 3076
  365.0 0.8 copy-start.6
  384.8 4.0 copy-start.24
  393.3 0.7 copy-start.22
  401.7 2.7 copy-start.5
  404.4 7.7 copy-start.17
  404.4 141.6 %copy-start.20 = (f32[1024]{0:T(1024)S(1)}, f32[1024]{0:T(1024)}, u32[]{:S(2)}) copy-start(f32[1024]{0:T(1024)} %copy-done.19) | copy-start | bytes 12292
  407.2 296.4 %all-to-all-start.1 = ((bf16[64,4,1024]{2,1,0:T(4,128)(2,1)}), bf16[64,4,1024]{2,1,0:T(4,128)(2,1)S(1)}, u32[]{:S(2)}, u32[]{:S(2)}) async-start(bf16[64,4,1024]{2,1,0:T(4,128)(2,1)} %fusion.47), calls=%async_computation.1 | async-start | bytes 1048576 | tf_op jit(solution)/shard_map/all_to_all | solution.py:106
  412.0 436.7 %all-reduce.6.cloned.1.call-start = ((), (), s32[]{:S(2)}) async-start(), calls=%async_computation.5 | async-start | bytes 131072 | tf_op jit(solution)/shard_map/psum | solution.py:110
  704.6 3.9 copy-start.10
  708.5 2.4 copy-start.2
  710.8 1.2 copy-start.4
  710.8 1.7 copy-start.12
  712.5 1.2 copy-start.13
  712.5 2.4 slice-start
  713.8 1.5 copy-start.8
  713.8 2.2 slice-start.1
  713.8 2.2 copy-start.30
  716.0 2.9 copy-start.26
  716.0 48.0 %copy-start.14 = (bf16[256,1024]{1,0:T(8,128)(2,1)S(1)}, bf16[256,1024]{1,0:T(8,128)(2,1)}, u32[]{:S(2)}) copy-start(bf16[256,1024]{1,0:T(8,128)(2,1)} %squeeze.21) | copy-start | bytes 1572868
  716.0 48.0 %copy-start.29 = (f32[256]{0:T(256)S(1)}, f32[256]{0:T(256)}, u32[]{:S(2)}) copy-start(f32[256]{0:T(256)} %copy-done.28) | copy-start | bytes 3076
Sparse Core Ops, SparseCore 0:
  12.1 128.8 all-gather.2
  393.4 370.5 reduce-scatter.1
  766.8 81.8 all-reduce.5
where the time goes:
time: 858 us; the launch traced here: 857 us
  blocking collectives  593 us (69%)
  waiting for transfers between devices  128 us (15%)
  matrix products  45.3 us (5%)
  local copies, waits for them, and re-layouts  30.5 us (4%)
  other arithmetic  24.6 us (3%)
  starting transfers between devices  20.1 us (2%)
  between operations  15.7 us (2%)
    unnamed x1, blocking collectives  157 us
    psum x1, blocking collectives, per_device(): mixed_err = lax.psum(jnp.sum(u_wide * w_v, axis=0), 'tm')  156 us
    all_gather x1, blocking collectives, per_device(): z = lax.all_gather(z, 'tm', axis=0, tiled=True)  148 us
    psum x1, blocking collectives, per_device(): u_mine = lax.psum(u_terms, ('env', 'tm'))  132 us
    psum x1, waiting for transfers between devices, per_device(): qk_grad = lax.psum(summed, 'env').astype(jnp.float32)  82.4 us
    reduce_scatter x1, waiting for transfers between devices, per_device(): summed = lax.psum_scatter(terms, 'tm', scatter_dimension=0, tiled=True)  45.1 us
  transfers between devices with their start and end apart: 5, of which 2 were waited for; matrix products, arithmetic and copies ran while one was open for 8% of the time, Pallas kernels for 0%

commit v1 on v0

--- a/solution.py
+++ b/solution.py
@@ -108,7 +108,7 @@
     u_terms = lax.dot_general(normed.astype(jnp.float32), t, (((0,), (0,)), ((), ())), precision=HI)
     summed = lax.psum_scatter(terms, "tm", scatter_dimension=0, tiled=True)
     qk_grad = lax.psum(summed, "env").astype(jnp.float32)
-    u_mine = lax.psum(u_terms, ("env", "tm"))
+    u_mine = lax.psum(lax.psum(u_terms, "env"), "tm")
     u_mine = lax.dynamic_slice_in_dim(u_mine, lax.axis_index("tm") * w_v.shape[0], w_v.shape[0], 0)
     u_wide = jnp.repeat(u_mine, size, axis=1)
     v_grad = u_wide * v

time: 858 us -> 1080 us (1.26)
  blocking collectives: 593 us -> 831 us
  waiting for transfers between devices: 128 us -> 107 us
    psum x1 -> x2, blocking collectives: 132 us -> 376 us  [per_device(): u_mine = lax.psum(lax.psum(u_terms, 'env'), 'tm')]
    reduce_scatter x1, waiting for transfers between devices: 45.1 us -> 0.02 us  [per_device(): summed = lax.psum_scatter(terms, 'tm', scatter_dimension=0, tiled=True)]
    psum x1, waiting for transfers between devices: 82.4 us -> 107 us  [per_device(): qk_grad = lax.psum(summed, 'env').astype(jnp.float32)]
  transfers between devices with their start and end apart: 5 -> 5, of which waited for: 2 -> 1; matrix products, arithmetic and copies ran while one was open for 8% -> 6% of each run, Pallas kernels for 0% -> 0%
where the time goes in v1:
time: 1080 us; the launch traced here: 1070 us
  blocking collectives  831 us (77%)
  waiting for transfers between devices  107 us (10%)
  matrix products  45.3 us (4%)
  local copies, waits for them, and re-layouts  30.4 us (3%)
  other arithmetic  24.6 us (2%)
  starting transfers between devices  20.1 us (2%)
  between operations  15.7 us (1%)
    psum x2, blocking collectives, per_device(): u_mine = lax.psum(lax.psum(u_terms, 'env'), 'tm')  376 us
    unnamed x1, blocking collectives  157 us
    psum x1, blocking collectives, per_device(): mixed_err = lax.psum(jnp.sum(u_wide * w_v, axis=0), 'tm')  150 us
    all_gather x1, blocking collectives, per_device(): z = lax.all_gather(z, 'tm', axis=0, tiled=True)  148 us
    psum x1, waiting for transfers between devices, per_device(): qk_grad = lax.psum(summed, 'env').astype(jnp.float32)  107 us
  transfers between devices with their start and end apart: 5, of which 1 were waited for; matrix products, arithmetic and copies ran while one was open for 6% of the time, Pallas kernels for 0%

profile of v1, /device:TPU:1, one launch (start us, length us, event | category | flops | bytes accessed | tf_op | source)
XLA Modules:
  0.0 1074.3 jit_solution(5468325328519251238)
XLA Ops:
  7.2 1.6 slice.24
  9.5 1.2 fusion.49
  10.7 0.5 copy-done.25
  11.3 4.9 convolution_convert_fusion
  16.1 1.1 slice_bitcast_fusion
  17.2 1.4 copy.98
  18.7 2.2 copy.97
  21.0 1.6 fusion.114
  23.3 0.7 copy-done.1
  24.0 1.0 copy-done.3
  25.4 0.7 fusion.37
  26.1 0.8 copy.135
  27.0 0.5 broadcast.202
  27.5 4.5 reduce.4
  32.0 2.2 reshape.279
  34.2 15.1 %all-to-all-start = ((bf16[64,2,2048]{2,1,0:T(2,128)(2,1)}), bf16[64,2,2048]{2,1,0:T(2,128)(2,1)S(1)}, u32[]{:S(2)}, u32[]{:S(2)}) async-start(bf16[64,2,2048]{2,1,0:T(2,128)(2,1)} %reshape.279), calls=%async_computation | async-start | bytes 1048576 | tf_op jit(solution)/shard_map/all_to_all | solution.py:102
  49.4 0.6 dynamic-slice
  51.0 156.9 %all-reduce.3 = f32[1024]{0:T(1024)S(1)} all-reduce(f32[1024]{0:T(1024)S(1)} %dynamic-update-slice), channel_id=1, replica_groups=mesh['env'=4,'tm'=64] {'tm'}, use_global_device_ids=true, to_apply=%add.3 | all-reduce | flops 1024 | bytes 8192
  207.9 0.8 fusion.93
  208.9 148.0 %all-gather = f32[64,16,8]{1,2,0:T(8,128)S(1)} all-gather(f32[1,16,8]{1,2,0:T(8,128)S(1)} %bitcast.169), channel_id=1, replica_groups=mesh['env'=4,'tm'=64] {'tm'}, dimensions={0}, use_global_device_ids=true | all-gather | bytes 33280 | tf_op jit(solution)/shard_map/all_gather | solution.py:97
  357.2 0.7 broadcast_or_fusion
  357.9 1.8 reshape.280
  359.7 1.6 fusion.39
  361.5 0.7 copy.75
  362.2 1.3 reshape.268
  363.5 1.5 multiply_convert_fusion
  365.0 0.8 copy-done.6
  365.8 1.3 convolution_bitcast_fusion.3
  367.1 3.5 fusion.16
  370.9 1.0 fusion.113
  371.9 3.5 multiply_reduce_fusion.2
  375.4 1.3 fusion.95
  376.7 3.3 convolution_bitcast_fusion
  380.0 3.4 convolution_bitcast_fusion.1
  383.5 1.3 maximum_convert_fusion
  384.8 1.7 copy.78
  386.4 2.3 convert_element_type.173
  388.7 4.6 convolution_convert_fusion.1
  393.5 0.5 copy-done.22
  394.1 1.6 multiply_reduce_fusion
  395.8 3.8 fusion.115
  399.6 2.1 fusion.40
  401.8 2.6 reshape.260
  404.4 2.8 fusion.47
  407.2 4.9 all-to-all-start.1
  412.1 1.5 convolution_bitcast_fusion.2
  413.6 66.0 %psum.29 = f32[1024,8]{0,1:T(8,128)S(1)} all-reduce(f32[1024,8]{0,1:T(8,128)S(1)} %convolution_bitcast_fusion.2), channel_id=1, replica_groups=mesh['env'=4,'tm'=64] {'env'}, use_global_device_ids=true, to_apply=%region_19.20 | all-reduce | flops 8192 | bytes 65536 | tf_op jit(solution)/shard_map/psum | solution.py:111
  479.5 310.0 %psum.30 = f32[1024,8]{0,1:T(8,128)S(1)} all-reduce(f32[1024,8]{0,1:T(8,128)S(1)} %psum.29), channel_id=1, replica_groups=mesh['env'=4,'tm'=64] {'tm'}, use_global_device_ids=true, to_apply=%region_20.21 | all-reduce | flops 8192 | bytes 65536 | tf_op jit(solution)/shard_map/psum | solution.py:111
  789.8 0.8 fusion.94
  790.5 150.2 %psum.31 = f32[1024]{0:T(1024)S(1)} all-reduce(f32[1024]{0:T(1024)S(1)} %get-tuple-element.19), channel_id=1, replica_groups=mesh['env'=4,'tm'=64] {'tm'}, use_global_device_ids=true, to_apply=%region_22.23 | all-reduce | flops 1024 | bytes 8192 | tf_op jit(solution)/shard_map/psum | solution.py:115
  940.8 0.7 broadcast_multiply_fusion
  941.5 0.9 squeeze.21
  942.4 2.6 convolution_convert_fusion.5
  945.1 1.2 copy.94
  946.3 2.3 fusion.6
  948.7 1.0 convert_reduce_fusion
  950.4 1.2 fusion.25
  951.7 1.2 fusion.24
  953.1 0.7 slice-done.1
  953.8 2.9 fusion.52
  956.8 2.3 fusion.67
  959.2 107.1 %all-reduce.6.cloned.1.call-done = bf16[16,2048]{1,0:T(8,128)(2,1)} async-done(((bf16[16,2048]{1,0:T(8,128)(2,1)}), bf16[16,2048]{1,0:T(8,128)(2,1)}) %all-reduce.6.cloned.1.call-update) | async-done | bytes 65552 | tf_op jit(solution)/shard_map/psum | solution.py:110
  1066.2 0.8 convert_element_type.192
  1067.1 0.7 pad_maximum_fusion
  (108 shorter events, 4.4 us)
Async XLA Ops:
  7.2 18.2 %copy-start = (bf16[1024,1024]{1,0:T(8,128)(2,1)S(1)}, bf16[1024,1024]{1,0:T(8,128)(2,1)}, u32[]{:S(2)}) copy-start(bf16[1024,1024]{1,0:T(8,128)(2,1)} %param.17) | copy-start | bytes 6291460
  7.2 359.9 %all-gather.3.cloned.1.call-start = ((), (), s32[]{:S(2)}) async-start(), calls=%async_computation.3 | async-start | bytes 4259840 | tf_op jit(solution)/shard_map/all_gather | solution.py:98
  10.7 0.5 copy-start.25
  11.3 4.9 copy-start.28
  17.2 6.8 copy-start.9
  18.7 3.9 copy-start.11
  22.6 1.4 copy-start.1
  22.9 2.4 copy-start.16
  22.9 2.4 copy-start.7
  24.0 1.0 copy-start.3
  26.9 22.4 %copy-start.31 = (u32[256]{0:T(256)S(1)}, u32[256]{0:T(256)}, u32[]{:S(2)}) copy-start(u32[256]{0:T(256)} %constant.61) | copy-start | bytes 3076
  26.9 23.7 %copy-start.18 = (f32[1024]{0:T(1024)S(1)}, f32[1024]{0:T(1024)}, u32[]{:S(2)}) copy-start(f32[1024]{0:T(1024)} %param.21) | copy-start | bytes 12292
  27.0 23.7 %copy-start.21 = (bf16[16,1024]{1,0:T(8,128)(2,1)S(1)}, bf16[16,1024]{1,0:T(8,128)(2,1)}, u32[]{:S(2)}) copy-start(bf16[16,1024]{1,0:T(8,128)(2,1)} %param.20) | copy-start | bytes 98308
  32.0 325.1 %copy-start.27 = (s32[1,64,4]{1,2,0:T(4,128)S(1)}, s32[1,64,4]{1,2,0:T(4,128)}, u32[]{:S(2)}) copy-start(s32[1,64,4]{1,2,0:T(4,128)} %param.13) | copy-start | bytes 3076
  34.2 323.7 %all-to-all-start = ((bf16[64,2,2048]{2,1,0:T(2,128)(2,1)}), bf16[64,2,2048]{2,1,0:T(2,128)(2,1)S(1)}, u32[]{:S(2)}, u32[]{:S(2)}) async-start(bf16[64,2,2048]{2,1,0:T(2,128)(2,1)} %reshape.279), calls=%async_computation | async-start | bytes 1048576 | tf_op jit(solution)/shard_map/all_to_all | solution.py:102
  49.3 907.5 %reduce-scatter.2.cloned.1.call-start = ((), (), s32[]{:S(2)}) async-start(), calls=%async_computation.4 | async-start | bytes 4259840 | tf_op jit(solution)/shard_map/reduce_scatter | solution.py:109
  207.9 149.2 %copy-start.19 = (f32[1024]{0:T(1024)}, f32[1024]{0:T(1024)S(1)}, u32[]{:S(2)}) copy-start(f32[1024]{0:T(1024)S(1)} %all-reduce.3) | copy-start | bytes 12292
  357.9 5.6 copy-start.15
  361.3 9.4 copy-start.23
  365.0 0.8 copy-start.6
  384.8 4.0 copy-start.24
  393.3 0.7 copy-start.22
  401.7 2.7 copy-start.5
  404.4 7.7 copy-start.17
  404.4 385.3 %copy-start.20 = (f32[1024]{0:T(1024)S(1)}, f32[1024]{0:T(1024)}, u32[]{:S(2)}) copy-start(f32[1024]{0:T(1024)} %copy-done.19) | copy-start | bytes 12292
  407.2 534.3 %all-to-all-start.1 = ((bf16[64,4,1024]{2,1,0:T(4,128)(2,1)}), bf16[64,4,1024]{2,1,0:T(4,128)(2,1)S(1)}, u32[]{:S(2)}, u32[]{:S(2)}) async-start(bf16[64,4,1024]{2,1,0:T(4,128)(2,1)} %fusion.47), calls=%async_computation.1 | async-start | bytes 1048576 | tf_op jit(solution)/shard_map/all_to_all | solution.py:106
  412.0 654.2 %all-reduce.6.cloned.1.call-start = ((), (), s32[]{:S(2)}) async-start(), calls=%async_computation.5 | async-start | bytes 131072 | tf_op jit(solution)/shard_map/psum | solution.py:110
  942.4 3.9 copy-start.10
  946.3 2.4 copy-start.2
  948.7 1.2 copy-start.4
  948.7 1.7 copy-start.12
  950.4 1.2 copy-start.13
  950.4 2.4 slice-start
  951.6 1.4 copy-start.8
  951.6 2.2 slice-start.1
  951.7 2.2 copy-start.30
  953.8 2.9 copy-start.26
  953.8 3.0 copy-start.14
  953.8 3.0 copy-start.29
Sparse Core Ops, SparseCore 0:
  12.1 128.8 all-gather.2
  393.4 369.1 reduce-scatter.1
  956.9 109.2 all-reduce.5
